TPU v7x, 32 devices: a whole 2x2x4 slice. The times are simulated.
32 devices in a mesh: dp: 16 (over z, y, core), head: 2 (over x).
Axes of the slice: x: 2, y: 2, z: 4, core: 2. Of those that a mesh axis runs over, the one named last changes fastest.
Arguments:
- tokens: bfloat16 [16, 256, 512], P('dp', 'head'), may hold values from -6 to 6
- lengths: int32 [16], P('dp'), may hold values from 32 to 256, as said below
- cotangent: bfloat16 [16, 256, 512], P('dp', 'head'), may hold values from -6 to 6
- glu_weight: bfloat16 [512, 1024], replicated, may hold values from -0.25 to 0.25
- glu_bias: bfloat16 [1024], replicated, may hold values from -1.75 to 1.75
- norm_gain: bfloat16 [4, 512], replicated, may hold values from 0.25 to 1.75
- norm_bias: bfloat16 [4, 512], replicated, may hold values from -1.75 to 1.75
- mid_gain: bfloat16 [2048], replicated, may hold values from 0.25 to 1.75
- mid_bias: bfloat16 [2048], replicated, may hold values from -1.75 to 1.75
- left_weight: bfloat16 [512, 2048], replicated, may hold values from -0.25 to 0.25
- left_bias: bfloat16 [2048], replicated, may hold values from -1.75 to 1.75
- conv_weight: bfloat16 [3, 512, 256], replicated, may hold values from -0.15625 to 0.15625
- conv_bias: bfloat16 [256], replicated, may hold values from -1.75 to 1.75
- depth_weight: bfloat16 [9, 2048], replicated, may hold values from -2 to 2
- point_weight: bfloat16 [2048, 256], replicated, may hold values from -0.125 to 0.125
- point_bias: bfloat16 [256], replicated, may hold values from -1.75 to 1.75
- qkv_weight: bfloat16 [512, 1536], replicated, may hold values from -0.375 to 0.375
- out_weight: bfloat16 [512, 512], replicated, may hold values from -1 to 1
- ffn_in_weight: bfloat16 [512, 2048], replicated, may hold values from -0.25 to 0.25
- ffn_in_bias: bfloat16 [2048], replicated, may hold values from -1.75 to 1.75
- ffn_out_weight: bfloat16 [2048, 512], replicated, may hold values from -0.125 to 0.125
- ffn_out_bias: bfloat16 [512], replicated, may hold values from -1.75 to 1.75
Outputs:
- out_tokens: bfloat16 [16, 256, 512], P('dp', 'head')
- grad_tokens: float32 [16, 256, 512], P('dp', 'head')
- grad_glu_weight: float32 [512, 1024], P('dp')
- grad_glu_bias: float32 [1024], P('dp')
- grad_norm_gain: float32 [4, 512], P(None, 'dp')
- grad_norm_bias: float32 [4, 512], P(None, 'dp')
- grad_mid_gain: float32 [2048], P('dp')
- grad_mid_bias: float32 [2048], P('dp')
- grad_left_weight: float32 [512, 2048], P('dp')
- grad_left_bias: float32 [2048], P('dp')
- grad_conv_weight: float32 [3, 512, 256], P(None, 'dp')
- grad_conv_bias: float32 [256], replicated
- grad_depth_weight: float32 [9, 2048], P(None, 'dp')
- grad_point_weight: float32 [2048, 256], P('dp')
- grad_point_bias: float32 [256], replicated
- grad_qkv_weight: float32 [512, 1536], P('dp')
- grad_out_weight: float32 [512, 512], P('dp')
- grad_ffn_in_weight: float32 [512, 2048], P('dp')
- grad_ffn_in_bias: float32 [2048], P('dp')
- grad_ffn_out_weight: float32 [2048, 512], P('dp')
- grad_ffn_out_bias: float32 [512], P('dp')
Inputs may be any that keep to these rules, and one draw needn't show every extreme that they name: `lengths`: counted from the start of the row; some row is full.
All inputs are finite; a program needn't handle non-finite values.
Results may differ from a plain program's by a relative error of at most 0.03.
The roundings to bfloat16 on the way count: a program that leaves them out, or rounds other values in their place, can miss the bound.
Values may be sent and summed in bfloat16 or wider, within the bound.
No kernel may reach another device: no remote copies, remote signals or barrier semaphores. Data moves between devices by JAX's collectives and lax.ppermute only.
A program may use at most 128 MiB of HBM per device.

v0:
```python
import jax
import jax.numpy as jnp
from jax import lax
from jax.sharding import PartitionSpec as P

HEAD_DIM = 64
EPSILON = 1e-06


def padded(cells, sides, width):
    for axis, dim in sides:
        count = lax.axis_size(axis)
        ends = count - 1
        head = lax.slice_in_dim(cells, 0, width, axis=dim)
        tail = lax.slice_in_dim(cells, cells.shape[dim] - width, cells.shape[dim], axis=dim)
        cells = jnp.concatenate(
            [
                lax.ppermute(tail, axis, [(i, (i + 1) % count) for i in range(ends)]),
                cells,
                lax.ppermute(head, axis, [((i + 1) % count, i) for i in range(ends)]),
            ],
            axis=dim,
        )
    return cells


def layer_norm(inputs, gain_vec, bias_vec):
    average = jnp.mean(inputs, axis=-1, keepdims=True)
    centred = inputs - average
    spread = jnp.mean(centred * centred, axis=-1, keepdims=True)
    return centred * lax.rsqrt(spread + EPSILON) * gain_vec + bias_vec


def project(inputs, weight):
    return jnp.dot(inputs, weight, preferred_element_type=jnp.float32)


def project_back(incoming, weight):
    return jnp.einsum("bte,de->btd", incoming, weight, preferred_element_type=jnp.float32)


def weight_grad(inputs, incoming):
    return jnp.einsum("btd,bte->de", inputs, incoming, preferred_element_type=jnp.float32)


def token_sum(incoming):
    return jnp.sum(incoming.astype(jnp.float32), axis=(0, 1))


def norm_back(inputs, gain_vec, bias_vec, incoming):
    unused, pullback = jax.vjp(layer_norm, inputs, gain_vec, bias_vec)
    return pullback(incoming)


def per_device(
    tokens,
    lengths,
    cotangent,
    glu_weight,
    glu_bias,
    norm_gain,
    norm_bias,
    mid_gain,
    mid_bias,
    left_weight,
    left_bias,
    conv_weight,
    conv_bias,
    depth_weight,
    point_weight,
    point_bias,
    qkv_weight,
    out_weight,
    ffn_in_weight,
    ffn_in_bias,
    ffn_out_weight,
    ffn_out_bias,
):
    row_count, part_len, width = tokens.shape
    groups = lax.axis_size("head")
    seq_len = part_len * groups
    local_width = width // groups
    local_heads = local_width // HEAD_DIM
    half_width = conv_weight.shape[2]
    ffn_width = left_weight.shape[1]
    scale = HEAD_DIM ** (-0.5)
    begin = lax.axis_index("head") * part_len
    places = begin + jnp.arange(part_len, dtype=jnp.int32)
    columns = (places[None, :] < lengths[:, None]).astype(jnp.float32)[:, :, None]
    keys_open = (jnp.arange(seq_len, dtype=jnp.int32)[None, :] < lengths[:, None])[:, None, None, :]
    gains = norm_gain.astype(jnp.float32)
    shifts = norm_bias.astype(jnp.float32)
    mid_gains = mid_gain.astype(jnp.float32)
    mid_shifts = mid_bias.astype(jnp.float32)
    taps = depth_weight.astype(jnp.float32)
    conv_flat = conv_weight.reshape(3 * width, half_width)
    stream_in = tokens.astype(jnp.float32)
    first_norm = layer_norm(stream_in, gains[0], shifts[0]).astype(jnp.bfloat16)
    joined = project(first_norm, glu_weight) + glu_bias.astype(jnp.float32)
    values_part = joined[..., :width]
    gate_part = jax.nn.sigmoid(joined[..., width:])
    after_glu = stream_in + values_part * gate_part
    second_norm = (layer_norm(after_glu, gains[1], shifts[1]) * columns).astype(jnp.bfloat16)
    left_pre = project(second_norm, left_weight) + left_bias.astype(jnp.float32)
    rimmed_second = padded(second_norm, (("head", 1),), 1)
    window = jnp.concatenate(
        [rimmed_second[:, :-2], rimmed_second[:, 1:-1], rimmed_second[:, 2:]], axis=-1
    )
    right_pre = project(window, conv_flat) + conv_bias.astype(jnp.float32)
    combined = jnp.where(left_pre > 0.0, left_pre, 0.0) + jnp.pad(
        jnp.where(right_pre > 0.0, right_pre, 0.0), ((0, 0), (0, 0), (0, ffn_width - half_width))
    )
    third_norm = layer_norm(combined, mid_gains, mid_shifts) * columns
    rimmed_third = padded(third_norm.astype(jnp.bfloat16), (("head", 1),), 4).astype(
        third_norm.dtype
    )
    depthwise = rimmed_third[:, 0:part_len] * taps[0]
    for offset in range(1, 9):
        depthwise = depthwise + rimmed_third[:, offset : offset + part_len] * taps[offset]
    depth_low = depthwise.astype(jnp.bfloat16)
    separable = project(depth_low, point_weight) + point_bias.astype(jnp.float32)
    after_conv = after_glu + jnp.pad(separable, ((0, 0), (0, 0), (0, width - half_width)))
    fourth_norm = layer_norm(after_conv, gains[2], shifts[2]).astype(jnp.bfloat16)
    packed = (
        project(fourth_norm, qkv_weight).astype(jnp.bfloat16).reshape(row_count, part_len, 3, width)
    )
    spread_out = lax.all_to_all(packed, "head", split_axis=3, concat_axis=1, tiled=True)
    shaped = spread_out.reshape(row_count, seq_len, 3, local_heads, HEAD_DIM)
    queries = shaped[:, :, 0]
    keyset = shaped[:, :, 1]
    valueset = shaped[:, :, 2]

    def masked_scores():
        raw_scores = (
            jnp.einsum("bqhd,bkhd->bhqk", queries, keyset, preferred_element_type=jnp.float32)
            * scale
        )
        return jnp.where(keys_open, raw_scores, -1000000000.0)

    scores = masked_scores()
    largest = jnp.max(scores, axis=-1, keepdims=True)
    raised = jnp.exp(scores - largest)
    totals = jnp.sum(raised, axis=-1, keepdims=True)
    log_total = largest + jnp.log(totals)
    context = jnp.einsum(
        "bhqk,bkhd->bqhd",
        (raised / totals).astype(jnp.bfloat16),
        valueset,
        preferred_element_type=jnp.float32,
    )
    context = context.astype(jnp.bfloat16).reshape(row_count, seq_len, local_width)
    returned = lax.all_to_all(context, "head", split_axis=1, concat_axis=2, tiled=True)
    after_attn = after_conv + project(returned, out_weight)
    fifth_norm = layer_norm(after_attn, gains[3], shifts[3]).astype(jnp.bfloat16)
    hidden_pre = project(fifth_norm, ffn_in_weight) + ffn_in_bias.astype(jnp.float32)
    hidden = jnp.where(hidden_pre > 0.0, hidden_pre, 0.0).astype(jnp.bfloat16)
    block_out = after_attn + project(hidden, ffn_out_weight) + ffn_out_bias.astype(jnp.float32)
    grad_stream = cotangent.astype(jnp.float32)
    g_ffn_out = weight_grad(hidden, cotangent)
    g_ffn_out_bias = token_sum(cotangent)
    d_hidden = jnp.where(hidden_pre > 0.0, project_back(cotangent, ffn_out_weight), 0.0).astype(
        jnp.bfloat16
    )
    g_ffn_in = weight_grad(fifth_norm, d_hidden)
    g_ffn_in_bias = token_sum(d_hidden)
    d_fifth, gain_three, shift_three = norm_back(
        after_attn, gains[3], shifts[3], project_back(d_hidden, ffn_in_weight)
    )
    d_after_attn = grad_stream + d_fifth
    d_attn = d_after_attn.astype(jnp.bfloat16)
    g_out = weight_grad(returned, d_attn)
    d_returned = project_back(d_attn, out_weight).astype(jnp.bfloat16)
    d_context = lax.all_to_all(d_returned, "head", split_axis=2, concat_axis=1, tiled=True)
    d_context = d_context.reshape(row_count, seq_len, local_heads, HEAD_DIM)
    probs = jnp.exp(masked_scores() - log_total)
    d_values = jnp.einsum(
        "bhqk,bqhd->bkhd", probs.astype(jnp.bfloat16), d_context, preferred_element_type=jnp.float32
    )
    d_probs = jnp.einsum("bqhd,bkhd->bhqk", d_context, valueset, preferred_element_type=jnp.float32)
    delta = jnp.sum(d_probs * probs, axis=-1, keepdims=True)
    d_scores = (probs * (d_probs - delta)).astype(jnp.bfloat16)
    d_queries = (
        jnp.einsum("bhqk,bkhd->bqhd", d_scores, keyset, preferred_element_type=jnp.float32) * scale
    )
    d_keys = (
        jnp.einsum("bhqk,bqhd->bkhd", d_scores, queries, preferred_element_type=jnp.float32) * scale
    )
    d_spread = jnp.stack([d_queries, d_keys, d_values], axis=2).astype(jnp.bfloat16)
    d_spread = d_spread.reshape(row_count, seq_len, 3, local_width)
    d_packed = lax.all_to_all(d_spread, "head", split_axis=1, concat_axis=3, tiled=True)
    d_packed = d_packed.reshape(row_count, part_len, 3 * width)
    g_qkv = weight_grad(fourth_norm, d_packed)
    upper = (g_ffn_out, g_ffn_out_bias, g_ffn_in, g_ffn_in_bias, g_out, g_qkv)
    d_fourth, gain_two, shift_two = norm_back(
        after_conv, gains[2], shifts[2], project_back(d_packed, qkv_weight)
    )
    d_after_conv = d_after_attn + d_fourth
    d_sep = d_after_conv[..., :half_width].astype(jnp.bfloat16)
    g_point = weight_grad(depth_low, d_sep)
    g_point_bias = token_sum(d_sep)
    d_depth = project_back(d_sep, point_weight)
    g_depth = jnp.stack(
        [
            jnp.sum(d_depth * rimmed_third[:, offset : offset + part_len], axis=(0, 1))
            for offset in range(9)
        ]
    )
    d_rimmed = padded(d_depth.astype(jnp.bfloat16), (("head", 1),), 4).astype(d_depth.dtype)
    d_third = d_rimmed[:, 8 : 8 + part_len] * taps[0]
    for offset in range(1, 9):
        d_third = d_third + d_rimmed[:, 8 - offset : 8 - offset + part_len] * taps[offset]
    d_third = d_third * columns
    d_combined, g_mid_gain, g_mid_bias = norm_back(combined, mid_gains, mid_shifts, d_third)
    d_left = jnp.where(left_pre > 0.0, d_combined, 0.0).astype(jnp.bfloat16)
    d_right = jnp.where(right_pre > 0.0, d_combined[..., :half_width], 0.0).astype(jnp.bfloat16)
    g_left = weight_grad(second_norm, d_left)
    g_left_bias = token_sum(d_left)
    g_conv = weight_grad(window, d_right).reshape(3, width, half_width)
    g_conv_bias = token_sum(d_right)
    d_window = project_back(d_right, conv_flat)
    side_taps = jnp.stack([d_window[..., :width], d_window[..., 2 * width :]], axis=0)
    side_rimmed = padded(side_taps.astype(jnp.bfloat16), (("head", 2),), 1).astype(side_taps.dtype)
    d_second = project_back(d_left, left_weight) + d_window[..., width : 2 * width]
    d_second = d_second + side_rimmed[0][:, 2:] + side_rimmed[1][:, :-2]
    d_second = d_second * columns
    d_norm_one, gain_one, shift_one = norm_back(after_glu, gains[1], shifts[1], d_second)
    d_after_glu = d_after_conv + d_norm_one
    d_values_part = d_after_glu * gate_part
    d_gate_part = d_after_glu * values_part * gate_part * (1.0 - gate_part)
    d_joined = jnp.concatenate([d_values_part, d_gate_part], axis=-1).astype(jnp.bfloat16)
    g_glu = weight_grad(first_norm, d_joined)
    g_glu_bias = token_sum(d_joined)
    d_norm_zero, gain_zero, shift_zero = norm_back(
        stream_in, gains[0], shifts[0], project_back(d_joined, glu_weight)
    )
    grad_input = d_after_glu + d_norm_zero
    g_gains = jnp.stack([gain_zero, gain_one, gain_two, gain_three])
    g_shifts = jnp.stack([shift_zero, shift_one, shift_two, shift_three])
    bias_totals = lax.psum((g_conv_bias, g_point_bias), ("dp", "head"))
    summed = (
        lax.psum_scatter(upper[0], "dp", scatter_dimension=0, tiled=True),
        lax.psum_scatter(upper[1], "dp", scatter_dimension=0, tiled=True),
        lax.psum_scatter(upper[2], "dp", scatter_dimension=0, tiled=True),
        lax.psum_scatter(upper[3], "dp", scatter_dimension=0, tiled=True),
        lax.psum_scatter(upper[4], "dp", scatter_dimension=0, tiled=True),
        lax.psum_scatter(upper[5], "dp", scatter_dimension=0, tiled=True),
        lax.psum_scatter(g_glu, "dp", scatter_dimension=0, tiled=True),
        lax.psum_scatter(g_glu_bias, "dp", scatter_dimension=0, tiled=True),
        lax.psum_scatter(g_gains, "dp", scatter_dimension=1, tiled=True),
        lax.psum_scatter(g_shifts, "dp", scatter_dimension=1, tiled=True),
        lax.psum_scatter(g_mid_gain, "dp", scatter_dimension=0, tiled=True),
        lax.psum_scatter(g_mid_bias, "dp", scatter_dimension=0, tiled=True),
        lax.psum_scatter(g_left, "dp", scatter_dimension=0, tiled=True),
        lax.psum_scatter(g_left_bias, "dp", scatter_dimension=0, tiled=True),
        lax.psum_scatter(g_conv, "dp", scatter_dimension=1, tiled=True),
        lax.psum_scatter(g_depth, "dp", scatter_dimension=1, tiled=True),
        lax.psum_scatter(g_point, "dp", scatter_dimension=0, tiled=True),
    )
    final = (
        lax.psum(summed[0].astype(jnp.bfloat16), "head").astype(jnp.float32),
        lax.psum(summed[1].astype(jnp.bfloat16), "head").astype(jnp.float32),
        lax.psum(summed[2].astype(jnp.bfloat16), "head").astype(jnp.float32),
        lax.psum(summed[3].astype(jnp.bfloat16), "head").astype(jnp.float32),
        lax.psum(summed[4].astype(jnp.bfloat16), "head").astype(jnp.float32),
        lax.psum(summed[5].astype(jnp.bfloat16), "head").astype(jnp.float32),
        lax.psum(summed[6].astype(jnp.bfloat16), "head").astype(jnp.float32),
        lax.psum(summed[7].astype(jnp.bfloat16), "head").astype(jnp.float32),
        lax.psum(summed[8].astype(jnp.bfloat16), "head").astype(jnp.float32),
        lax.psum(summed[9].astype(jnp.bfloat16), "head").astype(jnp.float32),
        lax.psum(summed[10].astype(jnp.bfloat16), "head").astype(jnp.float32),
        lax.psum(summed[11].astype(jnp.bfloat16), "head").astype(jnp.float32),
        lax.psum(summed[12].astype(jnp.bfloat16), "head").astype(jnp.float32),
        lax.psum(summed[13].astype(jnp.bfloat16), "head").astype(jnp.float32),
        lax.psum(summed[14].astype(jnp.bfloat16), "head").astype(jnp.float32),
        lax.psum(summed[15].astype(jnp.bfloat16), "head").astype(jnp.float32),
        lax.psum(summed[16].astype(jnp.bfloat16), "head").astype(jnp.float32),
    )
    return (
        block_out.astype(jnp.bfloat16),
        grad_input,
        final[6],
        final[7],
        final[8],
        final[9],
        final[10],
        final[11],
        final[12],
        final[13],
        final[14],
        bias_totals[0],
        final[15],
        final[16],
        bias_totals[1],
        final[5],
        final[4],
        final[2],
        final[3],
        final[0],
        final[1],
    )


def solution(mesh):
    return jax.shard_map(
        per_device,
        mesh=mesh,
        in_specs=(
            P("dp", "head", None),
            P("dp"),
            P("dp", "head", None),
            P(),
            P(),
            P(),
            P(),
            P(),
            P(),
            P(),
            P(),
            P(),
            P(),
            P(),
            P(),
            P(),
            P(),
            P(),
            P(),
            P(),
            P(),
            P(),
        ),
        out_specs=(
            P("dp", "head", None),
            P("dp", "head", None),
            P("dp", None),
            P("dp"),
            P(None, "dp"),
            P(None, "dp"),
            P("dp"),
            P("dp"),
            P("dp", None),
            P("dp"),
            P(None, "dp", None),
            P(),
            P(None, "dp"),
            P("dp", None),
            P(),
            P("dp", None),
            P("dp", None),
            P("dp", None),
            P("dp"),
            P("dp", None),
            P("dp"),
        ),
        check_vma=False,
    )
```

profile of v0, /device:TPU:0, one launch (start us, length us, event | category | flops | bytes accessed | tf_op | source)
XLA Modules:
  0.0 969.6 jit_solution(5460570614094923607)
XLA Ops:
  13.6 1.7 fusion.2
  17.2 5.0 collective-permute-start
  23.6 4.0 collective-permute-done.1
  30.0 1.7 collective-permute-start.2
  33.2 4.1 collective-permute-done.3
  41.5 1.9 copy.94
  43.5 2.1 copy.95
  45.6 4.2 all-to-all-start
  49.8 6.7 all-to-all-done
  58.8 2.0 reshape.963
  62.3 2.1 convolution_convert_fusion.3
  66.0 2.1 reduce.41
  69.6 4.0 all-to-all-start.1
  73.7 4.5 all-to-all-done.1
  79.9 1.7 copy.100
  83.3 2.1 convolution_add_fusion
  92.2 1.8 copy.101
  94.0 3.0 reduce.42
  98.6 4.0 all-to-all-start.2
  102.8 4.3 all-to-all-done.2
  107.1 1.7 reshape.991
  110.6 1.6 reshape.972
  112.3 1.8 multiply_reduce_fusion.2
  117.1 1.8 copy.106
  118.9 1.8 copy.107
  120.7 1.8 copy.108
  122.4 2.0 pad_maximum_fusion
  124.4 9.0 all_to_all.60
  134.2 1.9 copy.110
  136.2 3.0 fusion.65
  140.5 2.1 fusion.35
  144.0 2.5 collective-permute-start.4
  153.7 3.3 multiply_reduce_fusion
  159.6 3.8 collective-permute-start.6
  164.8 4.2 collective-permute-done.7
  176.0 2.1 stack.110
  180.5 2.0 copy.112
  182.4 2.5 fusion.87
  185.3 2.7 fusion.42
  188.1 1.9 fusion.68
  190.1 2.3 fusion.109
  193.5 2.8 fusion.106
  197.5 3.6 fusion.71
  201.1 3.8 fusion.39
  209.2 58.8 %all-reduce.9 = (bf16[1024]{0:T(1024)(128)(2,1)}, bf16[2048]{0:T(1024)(128)(2,1)}, bf16[2048]{0:T(1024)(128)(2,1)}, bf16[2048]{0:T(1024)(128)(2,1)}, bf16[2048]{0:T(1024)(128)(2,1)}, /*index=5*/bf16[512]{0:T(512)(128)(2,1)}) all-reduce(f32[1024]{0:T(1024)S(1)} %convert_reduce_fusion.2, ...), channel_id=3, replica_groups=mesh['dp'=16,'head'=2] {'dp'}, use_global_device_ids=true, to_apply=%region_26.27.clone | all-reduce | flops 9728 | bytes 58368
  277.0 10.3 %reduce-scatter.34.cloned.1.call-done = f32[32,4]{1,0:T(8,128)} async-done(((f32[512,4]{1,0:T(8,128)}), f32[32,4]{1,0:T(8,128)}) %reduce-scatter.34.cloned.1.call-update) | async-done | bytes 528
  288.6 53.8 %reduce-scatter.22.cloned.1.call-done = f32[9,128]{1,0:T(8,128)} async-done(((f32[9,2048]{1,0:T(8,128)}), f32[9,128]{1,0:T(8,128)}) %reduce-scatter.22.cloned.1.call-update) | async-done | bytes 4624 | tf_op jit(solution)/shard_map/reduce_scatter | solution.py:256
  343.7 59.1 %reduce-scatter.28.cloned.1.call-done = f32[32,512]{1,0:T(8,128)} async-done(((f32[512,512]{1,0:T(8,128)}), f32[32,512]{1,0:T(8,128)}) %reduce-scatter.28.cloned.1.call-update) | async-done | bytes 65552 | tf_op jit(solution)/shard_map/reduce_scatter | solution.py:245
  404.2 60.5 %reduce-scatter.20.cloned.1.call-done = f32[3,32,256]{2,1,0:T(8,128)} async-done(((f32[3,512,256]{2,1,0:T(8,128)}), f32[3,32,256]{2,1,0:T(8,128)}) %reduce-scatter.20.cloned.1.call-update) | async-done | bytes 98320 | tf_op jit(solution)/shard_map/reduce_scatter | solution.py:255
  467.0 62.3 %reduce-scatter.24.cloned.1.call-done = f32[128,256]{1,0:T(8,128)} async-done(((f32[2048,256]{1,0:T(8,128)}), f32[128,256]{1,0:T(8,128)}) %reduce-scatter.24.cloned.1.call-update) | async-done | bytes 131088 | tf_op jit(solution)/shard_map/reduce_scatter | solution.py:257
  530.9 62.8 %reduce-scatter.16.cloned.1.call-done = f32[32,1024]{1,0:T(8,128)} async-done(((f32[512,1024]{1,0:T(8,128)}), f32[32,1024]{1,0:T(8,128)}) %reduce-scatter.16.cloned.1.call-update) | async-done | bytes 131088 | tf_op jit(solution)/shard_map/reduce_scatter | solution.py:247
  595.2 68.0 %reduce-scatter.26.cloned.1.call-done = f32[32,1536]{1,0:T(8,128)} async-done(((f32[512,1536]{1,0:T(8,128)}), f32[32,1536]{1,0:T(8,128)}) %reduce-scatter.26.cloned.1.call-update) | async-done | bytes 196624 | tf_op jit(solution)/shard_map/reduce_scatter | solution.py:246
  664.8 74.4 %reduce-scatter.30.cloned.1.call-done = f32[32,2048]{1,0:T(8,128)} async-done(((f32[512,2048]{1,0:T(8,128)}), f32[32,2048]{1,0:T(8,128)}) %reduce-scatter.30.cloned.1.call-update) | async-done | bytes 262160 | tf_op jit(solution)/shard_map/reduce_scatter | solution.py:243
  739.2 1.6 convert_element_type.396
  740.8 73.6 %reduce-scatter.32.cloned.1.call-done = f32[128,512]{1,0:T(8,128)} async-done(((f32[2048,512]{1,0:T(8,128)}), f32[128,512]{1,0:T(8,128)}) %reduce-scatter.32.cloned.1.call-update) | async-done | bytes 262160 | tf_op jit(solution)/shard_map/reduce_scatter | solution.py:241
  814.4 1.6 convert_element_type.401
  816.0 74.6 %reduce-scatter.18.cloned.1.call-done = f32[32,2048]{1,0:T(8,128)} async-done(((f32[512,2048]{1,0:T(8,128)}), f32[32,2048]{1,0:T(8,128)}) %reduce-scatter.18.cloned.1.call-update) | async-done | bytes 262160 | tf_op jit(solution)/shard_map/reduce_scatter | solution.py:253
  890.6 1.6 convert_element_type.379
  894.3 40.0 %all-reduce.8 = (f32[256]{0:T(256)}, f32[256]{0:T(256)}) all-reduce(f32[256]{0:T(256)} %get-tuple-element.67, f32[256]{0:T(256)S(1)} %convert_reduce_fusion.5), channel_id=1, replica_groups=mesh['dp'=16,'head'=2] {'dp','head'}, use_global_device_ids=true, to_apply=%region_54.55 | all-reduce | flops 512 | bytes 4096 | tf_op jit(solution)/shard_map/psum | solution.py:239
  934.9 1.9 add_add_fusion.5
  950.2 3.4 all-reduce.17.cloned.1.call-done
  953.6 1.6 convert_element_type.380
  955.2 1.6 convert_element_type.397
  956.8 1.6 convert_element_type.402
  (423 shorter events, 109.1 us)
Async XLA Ops:
  7.2 78.2 %copy-start = (bf16[2048,512]{1,0:T(8,128)(2,1)S(1)}, bf16[2048,512]{1,0:T(8,128)(2,1)}, u32[]{:S(2)}) copy-start(bf16[2048,512]{1,0:T(8,128)(2,1)} %param.42) | copy-start | bytes 6291460
  7.2 8.1 copy-start.12
  7.2 16.3 %copy-start.122 = (bf16[256]{0:T(256)(128)(2,1)S(1)}, bf16[256]{0:T(256)(128)(2,1)}, u32[]{:S(2)}) copy-start(bf16[256]{0:T(256)(128)(2,1)} %param.34) | copy-start | bytes 1540
  7.2 16.3 %copy-start.108 = (bf16[2048]{0:T(1024)(128)(2,1)S(1)}, bf16[2048]{0:T(1024)(128)(2,1)}, u32[]{:S(2)}) copy-start(bf16[2048]{0:T(1024)(128)(2,1)} %param.32) | copy-start | bytes 12292
  7.2 16.3 %copy-start.109 = (bf16[2048]{0:T(1024)(128)(2,1)S(1)}, bf16[2048]{0:T(1024)(128)(2,1)}, u32[]{:S(2)}) copy-start(bf16[2048]{0:T(1024)(128)(2,1)} %param.29) | copy-start | bytes 12292
  7.2 16.3 %copy-start.110 = (bf16[2048]{0:T(1024)(128)(2,1)S(1)}, bf16[2048]{0:T(1024)(128)(2,1)}, u32[]{:S(2)}) copy-start(bf16[2048]{0:T(1024)(128)(2,1)} %param.30) | copy-start | bytes 12292
  7.3 20.4 %copy-start.51 = (bf16[3,512,256]{2,1,0:T(8,128)(2,1)S(1)}, bf16[3,512,256]{2,1,0:T(8,128)(2,1)}, u32[]{:S(2)}) copy-start(bf16[3,512,256]{2,1,0:T(8,128)(2,1)} %param.33) | copy-start | bytes 2359300
  8.5 15.1 %copy-start.71 = (f32[128]{0:T(128)}, f32[128]{0:T(128)S(1)}, u32[]{:S(2)}) copy-start(f32[128]{0:T(128)S(1)} %broadcast_multiply_fusion.4) | copy-start | bytes 1540
  10.1 17.9 %copy-start.80 = (f32[128]{0:T(128)}, f32[128]{0:T(128)S(1)}, u32[]{:S(2)}) copy-start(f32[128]{0:T(128)S(1)} %fusion.93) | copy-start | bytes 1540
  11.5 16.4 %copy-start.68 = (f32[1,512]{1,0:T(1,128)}, f32[1,512]{1,0:T(1,128)S(1)}, u32[]{:S(2)}) copy-start(f32[1,512]{1,0:T(1,128)S(1)} %get-tuple-element.112) | copy-start | bytes 6148
  12.9 10.6 %copy-start.78 = (f32[1,512]{1,0:T(1,128)}, f32[1,512]{1,0:T(1,128)S(1)}, u32[]{:S(2)}) copy-start(f32[1,512]{1,0:T(1,128)S(1)} %get-tuple-element.117) | copy-start | bytes 6148
  16.1 22.9 %copy-start.10 = (f32[1,128,512]{2,1,0:T(8,128)}, f32[1,128,512]{2,1,0:T(8,128)S(1)}, u32[]{:S(2)}) copy-start(f32[1,128,512]{2,1,0:T(8,128)S(1)} %get-tuple-element.86) | copy-start | bytes 786436
  16.1 13.1 %copy-start.100 = (f32[128]{0:T(128)}, f32[128]{0:T(128)S(1)}, u32[]{:S(2)}) copy-start(f32[128]{0:T(128)S(1)} %broadcast_multiply_fusion.3) | copy-start | bytes 1540
  16.3 7.2 copy-start.106
  17.0 11.6 %copy-start.37 = (bf16[512,2048]{1,0:T(8,128)(2,1)S(1)}, bf16[512,2048]{1,0:T(8,128)(2,1)}, u32[]{:S(2)}) copy-start(bf16[512,2048]{1,0:T(8,128)(2,1)} %param.31) | copy-start | bytes 6291460
  17.0 12.6 %copy-start.102 = (f32[128]{0:T(128)}, f32[128]{0:T(128)S(1)}, u32[]{:S(2)}) copy-start(f32[128]{0:T(128)S(1)} %compare_convert_fusion) | copy-start | bytes 1540
  17.2 12.1 %copy-start.43 = (bf16[1,128,512]{2,1,0:T(8,128)(2,1)}, bf16[1,128,512]{2,1,0:T(8,128)(2,1)S(1)}, u32[]{:S(2)}) copy-start(bf16[1,128,512]{2,1,0:T(8,128)(2,1)S(1)} %multiply_convert_fusion.4) | copy-start | bytes 393220
  17.2 6.4 collective-permute-start
  22.2 5.5 collective-permute-start.1
  29.3 8.2 copy-start.1
  30.0 3.1 collective-permute-start.2
  31.7 5.6 collective-permute-start.3
  39.5 99.6 %copy-start.85 = (f32[128]{0:T(128)}, f32[128]{0:T(128)S(1)}, u32[]{:S(2)}) copy-start(f32[128]{0:T(128)S(1)} %broadcast_multiply_fusion.2) | copy-start | bytes 1540
  39.7 99.5 %copy-start.96 = (f32[128]{0:T(128)}, f32[128]{0:T(128)S(1)}, u32[]{:S(2)}) copy-start(f32[128]{0:T(128)S(1)} %fusion.96) | copy-start | bytes 1540
  45.6 10.9 %all-to-all-start = ((bf16[1,128,3,512]{1,2,0,3:T(4,128)(2,1)}), bf16[1,128,3,512]{1,2,0,3:T(4,128)(2,1)}, u32[]{:S(2)}, u32[]{:S(2)}) async-start(bf16[1,128,3,512]{1,2,0,3:T(4,128)(2,1)} %copy.95), calls=%async_computation | async-start | bytes 1048576 | tf_op jit(solution)/shard_map/all_to_all | solution.py:127
  62.3 11.4 %copy-start.111 = (bf16[2048]{0:T(1024)(128)(2,1)S(1)}, bf16[2048]{0:T(1024)(128)(2,1)}, u32[]{:S(2)}) copy-start(bf16[2048]{0:T(1024)(128)(2,1)} %param.41) | copy-start | bytes 12292
  64.4 18.9 %copy-start.66 = (f32[1,512]{1,0:T(1,128)S(1)}, f32[1,512]{1,0:T(1,128)}, u32[]{:S(2)}) copy-start(f32[1,512]{1,0:T(1,128)} %get-tuple-element.110) | copy-start | bytes 6148
  64.4 18.9 %copy-start.76 = (f32[1,512]{1,0:T(1,128)S(1)}, f32[1,512]{1,0:T(1,128)}, u32[]{:S(2)}) copy-start(f32[1,512]{1,0:T(1,128)} %get-tuple-element.114) | copy-start | bytes 6148
  69.6 8.6 all-to-all-start.1
  98.6 8.6 all-to-all-start.2
  102.6 173.1 %reduce-scatter.36.cloned.1.call-start = ((), (), s32[]{:S(2)}) async-start(), calls=%async_computation.25 | async-start | bytes 278528
  142.6 11.1 %copy-start.2 = (f32[128,2048]{1,0:T(8,128)S(1)}, f32[128,2048]{1,0:T(8,128)}, u32[]{:S(2)}) copy-start(f32[128,2048]{1,0:T(8,128)} %copy-done.1) | copy-start | bytes 3145732
  142.6 11.1 %copy-start.27 = (f32[1,128,256]{2,1,0:T(8,128)S(1)}, f32[1,128,256]{2,1,0:T(8,128)}, u32[]{:S(2)}) copy-start(f32[1,128,256]{2,1,0:T(8,128)} %copy-done.26) | copy-start | bytes 393220
  144.0 7.0 collective-permute-start.4
  146.5 5.9 collective-permute-start.5
  158.5 10.6 %copy-start.20 = (bf16[1,128,2048]{2,1,0:T(8,128)(2,1)}, bf16[1,128,2048]{2,1,0:T(8,128)(2,1)S(1)}, u32[]{:S(2)}) copy-start(bf16[1,128,2048]{2,1,0:T(8,128)(2,1)S(1)} %get-tuple-element.70) | copy-start | bytes 1572868
  159.1 9.9 %copy-start.11 = (f32[1,128,512]{2,1,0:T(8,128)S(1)}, f32[1,128,512]{2,1,0:T(8,128)}, u32[]{:S(2)}) copy-start(f32[1,128,512]{2,1,0:T(8,128)} %copy-done.10) | copy-start | bytes 786436
  159.1 9.9 %copy-start.38 = (bf16[512,2048]{1,0:T(8,128)(2,1)S(1)}, bf16[512,2048]{1,0:T(8,128)(2,1)}, u32[]{:S(2)}) copy-start(bf16[512,2048]{1,0:T(8,128)(2,1)} %param.31) | copy-start | bytes 6291460
  159.1 10.0 %copy-start.69 = (f32[1,512]{1,0:T(1,128)S(1)}, f32[1,512]{1,0:T(1,128)}, u32[]{:S(2)}) copy-start(f32[1,512]{1,0:T(1,128)} %copy-done.68) | copy-start | bytes 6148
  159.1 10.0 %copy-start.101 = (f32[128]{0:T(128)S(1)}, f32[128]{0:T(128)}, u32[]{:S(2)}) copy-start(f32[128]{0:T(128)} %copy-done.100) | copy-start | bytes 1540
  159.2 10.0 %copy-start.103 = (f32[128]{0:T(128)S(1)}, f32[128]{0:T(128)}, u32[]{:S(2)}) copy-start(f32[128]{0:T(128)} %copy-done.102) | copy-start | bytes 1540
  159.2 10.0 %copy-start.107 = (f32[128]{0:T(128)S(1)}, f32[128]{0:T(128)}, u32[]{:S(2)}) copy-start(f32[128]{0:T(128)} %copy-done.106) | copy-start | bytes 1540
  159.6 5.1 collective-permute-start.6
  163.4 5.5 collective-permute-start.7
  170.6 17.5 %copy-start.34 = (bf16[1,128,512]{2,1,0:T(8,128)(2,1)}, bf16[1,128,512]{2,1,0:T(8,128)(2,1)S(1)}, u32[]{:S(2)}) copy-start(bf16[1,128,512]{2,1,0:T(8,128)(2,1)S(1)} %get-tuple-element.72) | copy-start | bytes 393220
  170.8 17.3 %copy-start.35 = (bf16[1,128,512]{2,1,0:T(8,128)(2,1)}, bf16[1,128,512]{2,1,0:T(8,128)(2,1)S(1)}, u32[]{:S(2)}) copy-start(bf16[1,128,512]{2,1,0:T(8,128)(2,1)S(1)} %multiply_convert_fusion.2) | copy-start | bytes 393220
  170.8 7.4 copy-start.45
  170.8 7.4 copy-start.48
  172.5 7.0 copy-start.24
  172.6 7.0 copy-start.44
  173.5 113.7 %reduce-scatter.34.cloned.1.call-start = ((), (), s32[]{:S(2)}) async-start(), calls=%async_computation.24 | async-start | bytes 278528
  175.9 166.5 %reduce-scatter.22.cloned.1.call-start = ((), (), s32[]{:S(2)}) async-start(), calls=%async_computation.18 | async-start | bytes 139264 | tf_op jit(solution)/shard_map/reduce_scatter | solution.py:256
  178.2 224.6 %reduce-scatter.28.cloned.1.call-start = ((), (), s32[]{:S(2)}) async-start(), calls=%async_computation.21 | async-start | bytes 1114112 | tf_op jit(solution)/shard_map/reduce_scatter | solution.py:245
  179.6 285.2 %reduce-scatter.20.cloned.1.call-start = ((), (), s32[]{:S(2)}) async-start(), calls=%async_computation.17 | async-start | bytes 1671168 | tf_op jit(solution)/shard_map/reduce_scatter | solution.py:255
  185.0 344.4 %reduce-scatter.24.cloned.1.call-start = ((), (), s32[]{:S(2)}) async-start(), calls=%async_computation.19 | async-start | bytes 2228224 | tf_op jit(solution)/shard_map/reduce_scatter | solution.py:257
  188.0 405.7 %reduce-scatter.16.cloned.1.call-start = ((), (), s32[]{:S(2)}) async-start(), calls=%async_computation.15 | async-start | bytes 2228224 | tf_op jit(solution)/shard_map/reduce_scatter | solution.py:247
  190.0 473.2 %reduce-scatter.26.cloned.1.call-start = ((), (), s32[]{:S(2)}) async-start(), calls=%async_computation.20 | async-start | bytes 3342336 | tf_op jit(solution)/shard_map/reduce_scatter | solution.py:246
  192.4 546.7 %reduce-scatter.30.cloned.1.call-start = ((), (), s32[]{:S(2)}) async-start(), calls=%async_computation.22 | async-start | bytes 4456448 | tf_op jit(solution)/shard_map/reduce_scatter | solution.py:243
  196.3 618.1 %reduce-scatter.32.cloned.1.call-start = ((), (), s32[]{:S(2)}) async-start(), calls=%async_computation.23 | async-start | bytes 4456448 | tf_op jit(solution)/shard_map/reduce_scatter | solution.py:241
  201.1 689.5 %reduce-scatter.18.cloned.1.call-start = ((), (), s32[]{:S(2)}) async-start(), calls=%async_computation.16 | async-start | bytes 4456448 | tf_op jit(solution)/shard_map/reduce_scatter | solution.py:253
  205.0 731.8 %all-reduce.15.cloned.1.call-start = ((), (), s32[]{:S(2)}) async-start(), calls=%async_computation.26 | async-start | bytes 182272 | tf_op jit(solution)/shard_map/psum | solution.py:267
  466.3 487.3 %all-reduce.17.cloned.1.call-start = ((), (), s32[]{:S(2)}) async-start(), calls=%async_computation.27 | async-start | bytes 1245184 | tf_op jit(solution)/shard_map/psum | solution.py:266
  892.2 42.7 %copy-start.73 = (f32[128]{0:T(128)S(1)}, f32[128]{0:T(128)}, u32[]{:S(2)}) copy-start(f32[128]{0:T(128)} %copy-done.71) | copy-start | bytes 1540
  892.2 42.7 %copy-start.82 = (f32[128]{0:T(128)S(1)}, f32[128]{0:T(128)}, u32[]{:S(2)}) copy-start(f32[128]{0:T(128)} %copy-done.80) | copy-start | bytes 1540
  (85 other events, 244.0 us)
Sparse Core Ops, SparseCore 0:
  173.7 55.6 reduce-scatter.35
  232.9 54.3 reduce-scatter.33
  291.2 51.1 reduce-scatter.21
  346.3 56.4 reduce-scatter.27
  406.3 58.3 reduce-scatter.19
  468.8 60.5 reduce-scatter.23
  533.1 60.5 reduce-scatter.15
  598.0 65.1 reduce-scatter.25
  667.6 71.5 reduce-scatter.29
  742.9 71.4 reduce-scatter.31
  818.7 71.8 reduce-scatter.17
  895.1 21.7 all-reduce.14
  921.3 32.2 all-reduce.16
where the time goes:
time: 973 us; the launch traced here: 970 us
  waiting for transfers between devices  632 us (65%)
  blocking collectives  108 us (11%)
  other arithmetic  68.7 us (7%)
  local copies, waits for them, and re-layouts  62.2 us (6%)
  matrix products  48.9 us (5%)
  starting transfers between devices  31.3 us (3%)
  between operations  18.4 us (2%)
    reduce_scatter x1, waiting for transfers between devices, per_device(): lax.psum_scatter(g_left, 'dp', scatter_dimension=0, tiled=True)  74.6 us
    reduce_scatter x1, waiting for transfers between devices, per_device(): lax.psum_scatter(upper[2], 'dp', scatter_dimension=0, tiled=True)  74.4 us
    reduce_scatter x1, waiting for transfers between devices, per_device(): lax.psum_scatter(upper[0], 'dp', scatter_dimension=0, tiled=True)  73.6 us
    reduce_scatter x1, waiting for transfers between devices, per_device(): lax.psum_scatter(upper[5], 'dp', scatter_dimension=0, tiled=True)  68 us
    reduce_scatter x1, waiting for transfers between devices, per_device(): lax.psum_scatter(g_glu, 'dp', scatter_dimension=0, tiled=True)  62.8 us
    reduce_scatter x1, waiting for transfers between devices, per_device(): lax.psum_scatter(g_point, 'dp', scatter_dimension=0, tiled=True)  62.3 us
    reduce_scatter x1, waiting for transfers between devices, per_device(): lax.psum_scatter(g_conv, 'dp', scatter_dimension=1, tiled=True)  60.5 us
    reduce_scatter x1, waiting for transfers between devices, per_device(): lax.psum_scatter(upper[4], 'dp', scatter_dimension=0, tiled=True)  59.1 us
  transfers between devices with their start and end apart: 24, of which 18 were waited for; matrix products, arithmetic and copies ran while one was open for 8% of the time, Pallas kernels for 0%

commit v1 on v0

--- a/solution.py
+++ b/solution.py
@@ -236,7 +236,7 @@
     grad_input = d_after_glu + d_norm_zero
     g_gains = jnp.stack([gain_zero, gain_one, gain_two, gain_three])
     g_shifts = jnp.stack([shift_zero, shift_one, shift_two, shift_three])
-    bias_totals = lax.psum((g_conv_bias, g_point_bias), ("dp", "head"))
+    bias_totals = lax.psum(lax.psum((g_conv_bias, g_point_bias), "dp"), "head")
     summed = (
         lax.psum_scatter(upper[0], "dp", scatter_dimension=0, tiled=True),
         lax.psum_scatter(upper[1], "dp", scatter_dimension=0, tiled=True),

time: 973 us -> 972 us (level)
  blocking collectives: 108 us -> 73.4 us
  waiting for transfers between devices: 632 us -> 665 us
    psum x1, blocking collectives: 40 us -> 5.61 us  [per_device(): bias_totals = lax.psum(lax.psum((g_conv_bias, g_point_bias), 'dp'), 'head')]
    psum x1, waiting for transfers between devices: 3.4 us -> 22.6 us  [per_device(): lax.psum(summed[6].astype(jnp.bfloat16), 'head').astype(jnp.float32)]
    psum x1, waiting for transfers between devices: 0.01 us -> 15.5 us  [per_device(): lax.psum(summed[7].astype(jnp.bfloat16), 'head').astype(jnp.float32)]
  transfers between devices with their start and end apart: 24 -> 24, of which waited for: 18 -> 19; matrix products, arithmetic and copies ran while one was open for 8% -> 8% of each run, Pallas kernels for 0% -> 0%
where the time goes in v1:
time: 972 us; the launch traced here: 969 us
  waiting for transfers between devices  665 us (68%)
  blocking collectives  73.4 us (8%)
  other arithmetic  69.4 us (7%)
  local copies, waits for them, and re-layouts  62.3 us (6%)
  matrix products  48.9 us (5%)
  starting transfers between devices  31.3 us (3%)
  between operations  18.4 us (2%)
    reduce_scatter x1, waiting for transfers between devices, per_device(): lax.psum_scatter(g_left, 'dp', scatter_dimension=0, tiled=True)  74.3 us
    reduce_scatter x1, waiting for transfers between devices, per_device(): lax.psum_scatter(upper[2], 'dp', scatter_dimension=0, tiled=True)  74.2 us
    reduce_scatter x1, waiting for transfers between devices, per_device(): lax.psum_scatter(upper[0], 'dp', scatter_dimension=0, tiled=True)  73.4 us
    reduce_scatter x1, waiting for transfers between devices, per_device(): lax.psum_scatter(upper[5], 'dp', scatter_dimension=0, tiled=True)  68 us
    reduce_scatter x1, waiting for transfers between devices, per_device(): lax.psum_scatter(g_glu, 'dp', scatter_dimension=0, tiled=True)  62.9 us
    reduce_scatter x1, waiting for transfers between devices, per_device(): lax.psum_scatter(g_point, 'dp', scatter_dimension=0, tiled=True)  62.4 us
    reduce_scatter x1, waiting for transfers between devices, per_device(): lax.psum_scatter(g_conv, 'dp', scatter_dimension=1, tiled=True)  60.6 us
    reduce_scatter x1, waiting for transfers between devices, per_device(): lax.psum_scatter(upper[4], 'dp', scatter_dimension=0, tiled=True)  59.1 us
  transfers between devices with their start and end apart: 24, of which 19 were waited for; matrix products, arithmetic and copies ran while one was open for 8% of the time, Pallas kernels for 0%

profile of v1, /device:TPU:0, one launch (start us, length us, event | category | flops | bytes accessed | tf_op | source)
XLA Modules:
  0.0 968.7 jit_solution(4105749904012410108)
XLA Ops:
  13.6 1.7 fusion.2
  17.2 5.0 collective-permute-start
  23.6 4.0 collective-permute-done.1
  30.0 1.7 collective-permute-start.2
  33.2 4.1 collective-permute-done.3
  41.5 1.9 copy.94
  43.5 2.1 copy.95
  45.6 4.2 all-to-all-start
  49.9 6.7 all-to-all-done
  58.8 2.0 reshape.963
  62.3 2.1 convolution_convert_fusion.3
  66.0 2.1 reduce.41
  69.7 4.0 all-to-all-start.1
  73.7 4.5 all-to-all-done.1
  79.9 1.7 copy.100
  83.3 2.1 convolution_add_fusion
  92.2 1.8 copy.101
  94.0 3.0 reduce.42
  98.6 4.0 all-to-all-start.2
  102.8 4.3 all-to-all-done.2
  107.1 1.7 reshape.991
  110.6 1.6 reshape.972
  112.3 1.8 multiply_reduce_fusion.2
  117.1 1.8 copy.106
  118.9 1.8 copy.107
  120.7 1.8 copy.108
  122.5 2.0 pad_maximum_fusion
  124.5 9.0 all_to_all.60
  134.3 1.9 copy.110
  136.2 3.0 fusion.65
  140.5 2.1 fusion.35
  144.0 2.5 collective-permute-start.4
  153.7 3.3 multiply_reduce_fusion
  159.7 3.8 collective-permute-start.6
  164.8 4.2 collective-permute-done.7
  176.0 2.1 stack.110
  180.5 2.0 copy.112
  182.4 2.5 fusion.87
  185.3 2.7 fusion.42
  188.1 1.9 fusion.68
  190.1 2.3 fusion.109
  193.5 2.8 fusion.106
  197.5 3.6 fusion.71
  201.2 3.8 fusion.39
  210.7 58.8 %all-reduce.8 = (bf16[1024]{0:T(1024)(128)(2,1)}, bf16[2048]{0:T(1024)(128)(2,1)}, bf16[2048]{0:T(1024)(128)(2,1)}, bf16[2048]{0:T(1024)(128)(2,1)}, f32[256]{0:...) all-reduce(f32[1024]{0:T(1024)S(1)} %convert_reduce_fusion.2, ...), channel_id=3, replica_groups=mesh['dp'=16,'head'=2] {'dp'}, use_global_device_ids=true, to_apply=%region_26.27.clone | all-reduce | flops 10240 | bytes 62464
  278.6 8.6 reduce-scatter.34.cloned.1.call-done
  288.6 53.9 %reduce-scatter.22.cloned.1.call-done = f32[9,128]{1,0:T(8,128)} async-done(((f32[9,2048]{1,0:T(8,128)}), f32[9,128]{1,0:T(8,128)}) %reduce-scatter.22.cloned.1.call-update) | async-done | bytes 4624 | tf_op jit(solution)/shard_map/reduce_scatter | solution.py:256
  343.7 59.1 %reduce-scatter.28.cloned.1.call-done = f32[32,512]{1,0:T(8,128)} async-done(((f32[512,512]{1,0:T(8,128)}), f32[32,512]{1,0:T(8,128)}) %reduce-scatter.28.cloned.1.call-update) | async-done | bytes 65552 | tf_op jit(solution)/shard_map/reduce_scatter | solution.py:245
  404.3 60.6 %reduce-scatter.20.cloned.1.call-done = f32[3,32,256]{2,1,0:T(8,128)} async-done(((f32[3,512,256]{2,1,0:T(8,128)}), f32[3,32,256]{2,1,0:T(8,128)}) %reduce-scatter.20.cloned.1.call-update) | async-done | bytes 98320 | tf_op jit(solution)/shard_map/reduce_scatter | solution.py:255
  467.1 62.4 %reduce-scatter.24.cloned.1.call-done = f32[128,256]{1,0:T(8,128)} async-done(((f32[2048,256]{1,0:T(8,128)}), f32[128,256]{1,0:T(8,128)}) %reduce-scatter.24.cloned.1.call-update) | async-done | bytes 131088 | tf_op jit(solution)/shard_map/reduce_scatter | solution.py:257
  531.0 62.9 %reduce-scatter.16.cloned.1.call-done = f32[32,1024]{1,0:T(8,128)} async-done(((f32[512,1024]{1,0:T(8,128)}), f32[32,1024]{1,0:T(8,128)}) %reduce-scatter.16.cloned.1.call-update) | async-done | bytes 131088 | tf_op jit(solution)/shard_map/reduce_scatter | solution.py:247
  595.4 68.0 %reduce-scatter.26.cloned.1.call-done = f32[32,1536]{1,0:T(8,128)} async-done(((f32[512,1536]{1,0:T(8,128)}), f32[32,1536]{1,0:T(8,128)}) %reduce-scatter.26.cloned.1.call-update) | async-done | bytes 196624 | tf_op jit(solution)/shard_map/reduce_scatter | solution.py:246
  665.0 74.2 %reduce-scatter.30.cloned.1.call-done = f32[32,2048]{1,0:T(8,128)} async-done(((f32[512,2048]{1,0:T(8,128)}), f32[32,2048]{1,0:T(8,128)}) %reduce-scatter.30.cloned.1.call-update) | async-done | bytes 262160 | tf_op jit(solution)/shard_map/reduce_scatter | solution.py:243
  739.2 1.6 convert_element_type.396
  740.8 73.4 %reduce-scatter.32.cloned.1.call-done = f32[128,512]{1,0:T(8,128)} async-done(((f32[2048,512]{1,0:T(8,128)}), f32[128,512]{1,0:T(8,128)}) %reduce-scatter.32.cloned.1.call-update) | async-done | bytes 262160 | tf_op jit(solution)/shard_map/reduce_scatter | solution.py:241
  814.2 1.6 convert_element_type.401
  815.9 74.3 %reduce-scatter.18.cloned.1.call-done = f32[32,2048]{1,0:T(8,128)} async-done(((f32[512,2048]{1,0:T(8,128)}), f32[32,2048]{1,0:T(8,128)}) %reduce-scatter.18.cloned.1.call-update) | async-done | bytes 262160 | tf_op jit(solution)/shard_map/reduce_scatter | solution.py:253
  892.9 5.6 all-reduce.9
  899.2 1.9 add_add_fusion.5
  901.1 15.5 %all-reduce.15.cloned.1.call-done = (bf16[64]{0:T(256)(128)(2,1)}, bf16[4,32]{1,0:T(4,128)(2,1)}, bf16[4,32]{1,0:T(4,128)(2,1)}, bf16[128]{0:T(256)(128)(2,1)}, ...) async-done(((bf16[64]{0:T(256)(128)(2,1)}, ...) | async-done | bytes 85968 | tf_op jit(solution)/shard_map/psum | solution.py:267
  930.0 22.6 %all-reduce.17.cloned.1.call-done = (bf16[32,1024]{1,0:T(8,128)(2,1)}, bf16[32,2048]{1,0:T(8,128)(2,1)}, bf16[128,256]{1,0:T(8,128)(2,1)}, bf16[32,1536]{1,0:T(8...) async-done(((bf16[32,1024]{1,0:T(8,128)(2,1)}, bf16[32,2048]{1,0:T(8,128)(2,1)}, bf16[128,256]{1,0:T(8,128)(2,1)}, bf16[32,1536]{1,0:T(8,128)(2,1)}, ...) | async-done | bytes 622608 | tf_op jit(solution)/shard_map/psum | solution.py:266
  952.7 1.6 convert_element_type.380
  954.3 1.6 convert_element_type.397
  955.9 1.6 convert_element_type.402
  (423 shorter events, 111.5 us)
Async XLA Ops:
  7.2 78.2 %copy-start = (bf16[2048,512]{1,0:T(8,128)(2,1)S(1)}, bf16[2048,512]{1,0:T(8,128)(2,1)}, u32[]{:S(2)}) copy-start(bf16[2048,512]{1,0:T(8,128)(2,1)} %param.42) | copy-start | bytes 6291460
  7.2 8.1 copy-start.12
  7.2 16.3 %copy-start.122 = (bf16[256]{0:T(256)(128)(2,1)S(1)}, bf16[256]{0:T(256)(128)(2,1)}, u32[]{:S(2)}) copy-start(bf16[256]{0:T(256)(128)(2,1)} %param.34) | copy-start | bytes 1540
  7.2 16.3 %copy-start.108 = (bf16[2048]{0:T(1024)(128)(2,1)S(1)}, bf16[2048]{0:T(1024)(128)(2,1)}, u32[]{:S(2)}) copy-start(bf16[2048]{0:T(1024)(128)(2,1)} %param.32) | copy-start | bytes 12292
  7.2 16.3 %copy-start.109 = (bf16[2048]{0:T(1024)(128)(2,1)S(1)}, bf16[2048]{0:T(1024)(128)(2,1)}, u32[]{:S(2)}) copy-start(bf16[2048]{0:T(1024)(128)(2,1)} %param.29) | copy-start | bytes 12292
  7.2 16.3 %copy-start.110 = (bf16[2048]{0:T(1024)(128)(2,1)S(1)}, bf16[2048]{0:T(1024)(128)(2,1)}, u32[]{:S(2)}) copy-start(bf16[2048]{0:T(1024)(128)(2,1)} %param.30) | copy-start | bytes 12292
  7.3 20.4 %copy-start.51 = (bf16[3,512,256]{2,1,0:T(8,128)(2,1)S(1)}, bf16[3,512,256]{2,1,0:T(8,128)(2,1)}, u32[]{:S(2)}) copy-start(bf16[3,512,256]{2,1,0:T(8,128)(2,1)} %param.33) | copy-start | bytes 2359300
  8.5 15.1 %copy-start.71 = (f32[128]{0:T(128)}, f32[128]{0:T(128)S(1)}, u32[]{:S(2)}) copy-start(f32[128]{0:T(128)S(1)} %broadcast_multiply_fusion.4) | copy-start | bytes 1540
  10.1 17.9 %copy-start.80 = (f32[128]{0:T(128)}, f32[128]{0:T(128)S(1)}, u32[]{:S(2)}) copy-start(f32[128]{0:T(128)S(1)} %fusion.93) | copy-start | bytes 1540
  11.5 16.4 %copy-start.68 = (f32[1,512]{1,0:T(1,128)}, f32[1,512]{1,0:T(1,128)S(1)}, u32[]{:S(2)}) copy-start(f32[1,512]{1,0:T(1,128)S(1)} %get-tuple-element.114) | copy-start | bytes 6148
  12.9 10.6 %copy-start.78 = (f32[1,512]{1,0:T(1,128)}, f32[1,512]{1,0:T(1,128)S(1)}, u32[]{:S(2)}) copy-start(f32[1,512]{1,0:T(1,128)S(1)} %get-tuple-element.119) | copy-start | bytes 6148
  16.1 23.0 %copy-start.10 = (f32[1,128,512]{2,1,0:T(8,128)}, f32[1,128,512]{2,1,0:T(8,128)S(1)}, u32[]{:S(2)}) copy-start(f32[1,128,512]{2,1,0:T(8,128)S(1)} %get-tuple-element.88) | copy-start | bytes 786436
  16.1 13.1 %copy-start.100 = (f32[128]{0:T(128)}, f32[128]{0:T(128)S(1)}, u32[]{:S(2)}) copy-start(f32[128]{0:T(128)S(1)} %broadcast_multiply_fusion.3) | copy-start | bytes 1540
  16.3 7.2 copy-start.106
  17.0 11.6 %copy-start.37 = (bf16[512,2048]{1,0:T(8,128)(2,1)S(1)}, bf16[512,2048]{1,0:T(8,128)(2,1)}, u32[]{:S(2)}) copy-start(bf16[512,2048]{1,0:T(8,128)(2,1)} %param.31) | copy-start | bytes 6291460
  17.0 12.6 %copy-start.102 = (f32[128]{0:T(128)}, f32[128]{0:T(128)S(1)}, u32[]{:S(2)}) copy-start(f32[128]{0:T(128)S(1)} %compare_convert_fusion) | copy-start | bytes 1540
  17.2 12.1 %copy-start.43 = (bf16[1,128,512]{2,1,0:T(8,128)(2,1)}, bf16[1,128,512]{2,1,0:T(8,128)(2,1)S(1)}, u32[]{:S(2)}) copy-start(bf16[1,128,512]{2,1,0:T(8,128)(2,1)S(1)} %multiply_convert_fusion.4) | copy-start | bytes 393220
  17.2 6.4 collective-permute-start
  22.2 5.5 collective-permute-start.1
  29.3 8.2 copy-start.1
  30.0 3.2 collective-permute-start.2
  31.7 5.6 collective-permute-start.3
  39.6 99.6 %copy-start.85 = (f32[128]{0:T(128)}, f32[128]{0:T(128)S(1)}, u32[]{:S(2)}) copy-start(f32[128]{0:T(128)S(1)} %broadcast_multiply_fusion.2) | copy-start | bytes 1540
  39.7 99.5 %copy-start.96 = (f32[128]{0:T(128)}, f32[128]{0:T(128)S(1)}, u32[]{:S(2)}) copy-start(f32[128]{0:T(128)S(1)} %fusion.96) | copy-start | bytes 1540
  45.6 10.9 %all-to-all-start = ((bf16[1,128,3,512]{1,2,0,3:T(4,128)(2,1)}), bf16[1,128,3,512]{1,2,0,3:T(4,128)(2,1)}, u32[]{:S(2)}, u32[]{:S(2)}) async-start(bf16[1,128,3,512]{1,2,0,3:T(4,128)(2,1)} %copy.95), calls=%async_computation | async-start | bytes 1048576 | tf_op jit(solution)/shard_map/all_to_all | solution.py:127
  62.3 11.4 %copy-start.111 = (bf16[2048]{0:T(1024)(128)(2,1)S(1)}, bf16[2048]{0:T(1024)(128)(2,1)}, u32[]{:S(2)}) copy-start(bf16[2048]{0:T(1024)(128)(2,1)} %param.41) | copy-start | bytes 12292
  64.4 18.9 %copy-start.66 = (f32[1,512]{1,0:T(1,128)S(1)}, f32[1,512]{1,0:T(1,128)}, u32[]{:S(2)}) copy-start(f32[1,512]{1,0:T(1,128)} %get-tuple-element.112) | copy-start | bytes 6148
  64.4 18.9 %copy-start.76 = (f32[1,512]{1,0:T(1,128)S(1)}, f32[1,512]{1,0:T(1,128)}, u32[]{:S(2)}) copy-start(f32[1,512]{1,0:T(1,128)} %get-tuple-element.116) | copy-start | bytes 6148
  69.7 8.6 all-to-all-start.1
  98.6 8.6 all-to-all-start.2
  102.6 174.6 %reduce-scatter.36.cloned.1.call-start = ((), (), s32[]{:S(2)}) async-start(), calls=%async_computation.25 | async-start | bytes 278528
  142.6 11.1 %copy-start.2 = (f32[128,2048]{1,0:T(8,128)S(1)}, f32[128,2048]{1,0:T(8,128)}, u32[]{:S(2)}) copy-start(f32[128,2048]{1,0:T(8,128)} %copy-done.1) | copy-start | bytes 3145732
  142.6 11.1 %copy-start.27 = (f32[1,128,256]{2,1,0:T(8,128)S(1)}, f32[1,128,256]{2,1,0:T(8,128)}, u32[]{:S(2)}) copy-start(f32[1,128,256]{2,1,0:T(8,128)} %copy-done.26) | copy-start | bytes 393220
  144.0 7.0 collective-permute-start.4
  146.5 5.9 collective-permute-start.5
  158.5 10.6 %copy-start.20 = (bf16[1,128,2048]{2,1,0:T(8,128)(2,1)}, bf16[1,128,2048]{2,1,0:T(8,128)(2,1)S(1)}, u32[]{:S(2)}) copy-start(bf16[1,128,2048]{2,1,0:T(8,128)(2,1)S(1)} %get-tuple-element.72) | copy-start | bytes 1572868
  159.1 9.9 %copy-start.11 = (f32[1,128,512]{2,1,0:T(8,128)S(1)}, f32[1,128,512]{2,1,0:T(8,128)}, u32[]{:S(2)}) copy-start(f32[1,128,512]{2,1,0:T(8,128)} %copy-done.10) | copy-start | bytes 786436
  159.2 9.9 %copy-start.38 = (bf16[512,2048]{1,0:T(8,128)(2,1)S(1)}, bf16[512,2048]{1,0:T(8,128)(2,1)}, u32[]{:S(2)}) copy-start(bf16[512,2048]{1,0:T(8,128)(2,1)} %param.31) | copy-start | bytes 6291460
  159.2 10.0 %copy-start.69 = (f32[1,512]{1,0:T(1,128)S(1)}, f32[1,512]{1,0:T(1,128)}, u32[]{:S(2)}) copy-start(f32[1,512]{1,0:T(1,128)} %copy-done.68) | copy-start | bytes 6148
  159.2 10.0 %copy-start.101 = (f32[128]{0:T(128)S(1)}, f32[128]{0:T(128)}, u32[]{:S(2)}) copy-start(f32[128]{0:T(128)} %copy-done.100) | copy-start | bytes 1540
  159.2 10.0 %copy-start.103 = (f32[128]{0:T(128)S(1)}, f32[128]{0:T(128)}, u32[]{:S(2)}) copy-start(f32[128]{0:T(128)} %copy-done.102) | copy-start | bytes 1540
  159.2 10.0 %copy-start.107 = (f32[128]{0:T(128)S(1)}, f32[128]{0:T(128)}, u32[]{:S(2)}) copy-start(f32[128]{0:T(128)} %copy-done.106) | copy-start | bytes 1540
  159.7 5.1 collective-permute-start.6
  163.4 5.5 collective-permute-start.7
  170.6 17.5 %copy-start.34 = (bf16[1,128,512]{2,1,0:T(8,128)(2,1)}, bf16[1,128,512]{2,1,0:T(8,128)(2,1)S(1)}, u32[]{:S(2)}) copy-start(bf16[1,128,512]{2,1,0:T(8,128)(2,1)S(1)} %get-tuple-element.74) | copy-start | bytes 393220
  170.8 17.3 %copy-start.35 = (bf16[1,128,512]{2,1,0:T(8,128)(2,1)}, bf16[1,128,512]{2,1,0:T(8,128)(2,1)S(1)}, u32[]{:S(2)}) copy-start(bf16[1,128,512]{2,1,0:T(8,128)(2,1)S(1)} %multiply_convert_fusion.2) | copy-start | bytes 393220
  170.8 7.4 copy-start.45
  170.8 7.4 copy-start.48
  172.6 7.0 copy-start.24
  172.6 7.0 copy-start.44
  173.6 113.7 %reduce-scatter.34.cloned.1.call-start = ((), (), s32[]{:S(2)}) async-start(), calls=%async_computation.24 | async-start | bytes 278528
  175.9 166.5 %reduce-scatter.22.cloned.1.call-start = ((), (), s32[]{:S(2)}) async-start(), calls=%async_computation.18 | async-start | bytes 139264 | tf_op jit(solution)/shard_map/reduce_scatter | solution.py:256
  178.2 224.6 %reduce-scatter.28.cloned.1.call-start = ((), (), s32[]{:S(2)}) async-start(), calls=%async_computation.21 | async-start | bytes 1114112 | tf_op jit(solution)/shard_map/reduce_scatter | solution.py:245
  179.6 285.3 %reduce-scatter.20.cloned.1.call-start = ((), (), s32[]{:S(2)}) async-start(), calls=%async_computation.17 | async-start | bytes 1671168 | tf_op jit(solution)/shard_map/reduce_scatter | solution.py:255
  185.0 344.5 %reduce-scatter.24.cloned.1.call-start = ((), (), s32[]{:S(2)}) async-start(), calls=%async_computation.19 | async-start | bytes 2228224 | tf_op jit(solution)/shard_map/reduce_scatter | solution.py:257
  188.0 405.9 %reduce-scatter.16.cloned.1.call-start = ((), (), s32[]{:S(2)}) async-start(), calls=%async_computation.15 | async-start | bytes 2228224 | tf_op jit(solution)/shard_map/reduce_scatter | solution.py:247
  190.0 473.4 %reduce-scatter.26.cloned.1.call-start = ((), (), s32[]{:S(2)}) async-start(), calls=%async_computation.20 | async-start | bytes 3342336 | tf_op jit(solution)/shard_map/reduce_scatter | solution.py:246
  192.5 546.7 %reduce-scatter.30.cloned.1.call-start = ((), (), s32[]{:S(2)}) async-start(), calls=%async_computation.22 | async-start | bytes 4456448 | tf_op jit(solution)/shard_map/reduce_scatter | solution.py:243
  196.3 618.0 %reduce-scatter.32.cloned.1.call-start = ((), (), s32[]{:S(2)}) async-start(), calls=%async_computation.23 | async-start | bytes 4456448 | tf_op jit(solution)/shard_map/reduce_scatter | solution.py:241
  201.1 689.1 %reduce-scatter.18.cloned.1.call-start = ((), (), s32[]{:S(2)}) async-start(), calls=%async_computation.16 | async-start | bytes 4456448 | tf_op jit(solution)/shard_map/reduce_scatter | solution.py:253
  205.0 711.6 %all-reduce.15.cloned.1.call-start = ((), (), s32[]{:S(2)}) async-start(), calls=%async_computation.26 | async-start | bytes 182272 | tf_op jit(solution)/shard_map/psum | solution.py:267
  466.4 486.3 %all-reduce.17.cloned.1.call-start = ((), (), s32[]{:S(2)}) async-start(), calls=%async_computation.27 | async-start | bytes 1245184 | tf_op jit(solution)/shard_map/psum | solution.py:266
  891.8 7.4 copy-start.73
  891.8 7.4 copy-start.82
  (85 other events, 245.6 us)
Sparse Core Ops, SparseCore 0:
  173.7 55.5 reduce-scatter.35
  232.8 54.3 reduce-scatter.33
  291.2 51.2 reduce-scatter.21
  346.4 56.4 reduce-scatter.27
  406.3 58.4 reduce-scatter.19
  468.9 60.5 reduce-scatter.23
  533.2 60.5 reduce-scatter.15
  598.2 65.1 reduce-scatter.25
  667.8 71.3 reduce-scatter.29
  742.9 71.3 reduce-scatter.31
  818.6 71.5 reduce-scatter.17
  894.7 21.8 all-reduce.14
  920.9 31.6 all-reduce.16
